TPU v7x, 128 devices: a whole 4x4x4 slice. The times are simulated.
128 devices in a mesh: grp: 4 (over z_hi, core), blk: 32 (over x, z_lo, y).
Axes of the slice: x: 4, y: 4, z: 4 (z_hi: 2, z_lo: 2; z = z_hi * 2 + z_lo), core: 2. Of those that a mesh axis runs over, the one named last changes fastest.
Arguments:
- integrals: bfloat16 [32768, 32768], P('blk', 'grp'), may hold values from -0.046875 to 0.046875
- block_mask: int32 [256, 256], P('blk', 'grp'), may hold values from 0 to 1, as said below
- amplitudes: bfloat16 [32768, 1024], P(('grp', 'blk')), may hold values from -6 to 6
- pair_batches: int32 [8], replicated, may hold values from 0 to 7, each once
Outputs:
- ladder: bfloat16 [1024, 32768], P('grp', 'blk')
Inputs may be any that keep to these rules, and one draw needn't show every extreme that they name: `block_mask`: 0 or 1; the share of kept tiles rises from about a quarter in the first tile row to about three quarters in the last. `pair_batches`: each batch number once.
All inputs are finite; a program needn't handle non-finite values.
Results may differ from a plain program's by a relative error of at most 0.001.
Values may be sent and summed in bfloat16 or wider, within the bound.
No kernel may reach another device: no remote copies, remote signals or barrier semaphores. Data moves between devices by JAX's collectives and lax.ppermute only.
A program may use at most 128 MiB of HBM per device.

v0:
```python
import jax
import jax.numpy as jnp
from jax import lax
from jax.sharding import PartitionSpec as P

BLOCK = 128
BATCH = 128
NB = 8


def on_device(integrals, block_mask, amplitudes, pair_batches):
    rows_in = amplitudes.shape[0]
    grouped = amplitudes.reshape(rows_in, NB, BATCH)
    selector = (pair_batches[:, None] == jnp.arange(NB, dtype=jnp.int32)[None, :]).astype(
        jnp.bfloat16
    )
    picked = jnp.einsum("rnb,mn->rmb", grouped, selector, preferred_element_type=jnp.float32)
    chosen = picked.astype(jnp.bfloat16).reshape(rows_in, NB * BATCH)
    out_rows = integrals.shape[0]
    fragment = lax.all_gather(chosen, "blk", axis=0, tiled=True)
    number = fragment.shape[0]
    mcols = block_mask.astype(jnp.bfloat16)
    tiled = (
        integrals.reshape(out_rows // BLOCK, BLOCK, number // BLOCK, BLOCK)
        * mcols[:, None, :, None]
    )
    masked = tiled.reshape(out_rows, number)
    partial_sum = lax.dot_general(
        fragment, masked, (((0,), (1,)), ((), ())), preferred_element_type=jnp.float32
    )
    owned = lax.psum_scatter(partial_sum, "grp", scatter_dimension=0, tiled=True)
    return owned.astype(jnp.bfloat16)


def solution(mesh):
    in_specs = (P("blk", "grp"), P("blk", "grp"), P(("grp", "blk"), None), P())
    out_specs = P("grp", "blk")
    return jax.shard_map(
        on_device, mesh=mesh, in_specs=in_specs, out_specs=out_specs, check_vma=False
    )
```

profile of v0, /device:TPU:1, one launch (start us, length us, event | category | flops | bytes accessed | tf_op | source)
XLA Modules:
  0.0 298.4 jit_solution(4227521799634697145)
XLA Ops:
  6.5 0.0 all-gather.2.cloned.1.call-start
  6.5 1.1 copy.5
  7.7 1.0 convolution_convert_fusion
  8.7 0.9 copy.13
  9.6 0.0 all-gather.2.cloned.1.call-update
  9.6 0.0 reduce-scatter.2.cloned.1.call-start
  9.7 0.7 convert_element_type.15
  10.3 192.8 %all-gather.2.cloned.1.call-done = bf16[8192,1024]{1,0:T(8,128)(2,1)} async-done(((bf16[256,1024]{1,0:T(8,128)(2,1)}), bf16[8192,1024]{1,0:T(8,128)(2,1)}) %all-gather.2.cloned.1.call-update) | async-done | bytes 16777232 | tf_op jit(solution)/shard_map/all_gather | solution.py:20
  203.2 6.5 %mul.11 = bf16[8,128,64,128]{3,2,1,0:T(8,128)(2,1)} broadcast(bf16[8,64]{1,0:T(8,128)(2,1)S(1)} %convert_element_type.15), dimensions={0,2} | broadcast | bytes 16778240 | tf_op jit(solution)/shard_map/mul | solution.py:24
  209.6 29.5 %fusion = f32[1024,1024]{1,0:T(8,128)} fusion(bf16[8192,1024]{1,0:T(8,128)(2,1)} %all-gather.2.cloned.1.call-done, bf16[1024,8192]{1,0:T(8,128)(2,1)} %param.4, bf16[128,8,64,128]{3,2,1,0:T(8,128)(2,1)} %bitcast.17), kind=kOutput, calls=%fused_computation.1 | convolution fusion | flops 17188257792 | bytes 54525952 | tf_op jit(solution)/shard_map/dot_general | solution.py:28
  239.1 0.0 reduce-scatter.2.cloned.1.call-update
  239.1 50.3 %reduce-scatter.2.cloned.1.call-done = f32[256,1024]{1,0:T(8,128)} async-done(((f32[1024,1024]{1,0:T(8,128)}), f32[256,1024]{1,0:T(8,128)}) %reduce-scatter.2.cloned.1.call-update) | async-done | bytes 1048592 | tf_op jit(solution)/shard_map/reduce_scatter | solution.py:31
  289.5 2.1 convert_element_type.16
Async XLA Ops:
  6.5 196.6 %all-gather.2.cloned.1.call-start = ((), (), s32[]{:S(2)}) async-start(), calls=%async_computation.1 | async-start | bytes 17301504 | tf_op jit(solution)/shard_map/all_gather | solution.py:20
  9.6 279.9 %reduce-scatter.2.cloned.1.call-start = ((), (), s32[]{:S(2)}) async-start(), calls=%async_computation.2 | async-start | bytes 5242880 | tf_op jit(solution)/shard_map/reduce_scatter | solution.py:31
Sparse Core Ops, SparseCore 0:
  9.7 193.3 all-gather.1
  239.3 50.1 reduce-scatter.1
where the time goes:
time: 299 us; the launch traced here: 298 us
  waiting for transfers between devices  243 us (81%)
  matrix products  30.5 us (10%)
  between operations  13.4 us (4%)
  local copies, waits for them, and re-layouts  8.49 us (3%)
    all_gather x1, waiting for transfers between devices, on_device(): fragment = lax.all_gather(chosen, 'blk', axis=0, tiled=True)  193 us
    reduce_scatter x1, waiting for transfers between devices, on_device(): lax.psum_scatter(partial_sum, 'grp', scatter_dimension=0, tiled=True)  50.3 us
    dot_general x1, matrix products, on_device(): lax.dot_general(fragment, masked, (((0,), (1,)), ((), ())), preferred_ele...  29.5 us
    mul x1, local copies, waits for them, and re-layouts, on_device(): integrals.reshape(out_rows // BLOCK, BLOCK, number // BLOCK, BLOCK)  6.47 us
  transfers between devices with their start and end apart: 2, of which 2 were waited for; matrix products, arithmetic and copies ran while one was open for 0% of the time, Pallas kernels for 0%

commit v1 on v0

--- a/solution.py
+++ b/solution.py
@@ -17,7 +17,10 @@
     picked = jnp.einsum("rnb,mn->rmb", grouped, selector, preferred_element_type=jnp.float32)
     chosen = picked.astype(jnp.bfloat16).reshape(rows_in, NB * BATCH)
     out_rows = integrals.shape[0]
-    fragment = lax.all_gather(chosen, "blk", axis=0, tiled=True)
+    size = lax.axis_size("blk")
+    blocks = jnp.stack([chosen for _ in range(size)])
+    blocks = lax.all_to_all(blocks, "blk", split_axis=0, concat_axis=0)
+    fragment = jnp.concatenate(blocks, axis=0)
     number = fragment.shape[0]
     mcols = block_mask.astype(jnp.bfloat16)
     tiled = (

time: 299 us -> 457 us (1.53)
  waiting for transfers between devices: 243 us -> 387 us
  starting transfers between devices: 0.04 us -> 9.51 us
  local copies, waits for them, and re-layouts: 8.49 us -> 13.7 us
    all_to_all x0 -> x1, waiting for transfers between devices: none -> 306 us  [on_device(): blocks = lax.all_to_all(blocks, 'blk', split_axis=0, concat_axis=0)]
    all_gather x1 -> x0, waiting for transfers between devices: 193 us -> none  [on_device(): fragment = lax.all_gather(chosen, 'blk', axis=0, tiled=True)]
    reduce_scatter x1, waiting for transfers between devices: 50.3 us -> 80.7 us  [on_device(): lax.psum_scatter(partial_sum, 'grp', scatter_dimension=0, tiled=True)]
    all_to_all x0 -> x1, starting transfers between devices: none -> 9.47 us  [on_device(): blocks = lax.all_to_all(blocks, 'blk', split_axis=0, concat_axis=0)]
    another operation x0 -> x1, local copies, waits for them, and re-layouts: none -> 5.97 us  [on_device(): blocks = jnp.stack([chosen for _ in range(size)])]
where the time goes in v1:
time: 457 us; the launch traced here: 456 us
  waiting for transfers between devices  387 us (85%)
  matrix products  30.5 us (7%)
  local copies, waits for them, and re-layouts  13.7 us (3%)
  between operations  13.4 us (3%)
  starting transfers between devices  9.51 us (2%)
    all_to_all x1, waiting for transfers between devices, on_device(): blocks = lax.all_to_all(blocks, 'blk', split_axis=0, concat_axis=0)  306 us
    reduce_scatter x1, waiting for transfers between devices, on_device(): lax.psum_scatter(partial_sum, 'grp', scatter_dimension=0, tiled=True)  80.7 us
    dot_general x1, matrix products, on_device(): lax.dot_general(fragment, masked, (((0,), (1,)), ((), ())), preferred_ele...  29.5 us
    all_to_all x1, starting transfers between devices, on_device(): blocks = lax.all_to_all(blocks, 'blk', split_axis=0, concat_axis=0)  9.47 us
  transfers between devices with their start and end apart: 2, of which 2 were waited for; matrix products, arithmetic and copies ran while one was open for 0% of the time, Pallas kernels for 0%

profile of v1, /device:TPU:1, one launch (start us, length us, event | category | flops | bytes accessed | tf_op | source)
XLA Modules:
  0.0 456.2 jit_solution(16161924259358618020)
XLA Ops:
  6.5 1.1 copy.5
  7.7 1.0 convolution_convert_fusion
  8.7 0.1 copy.13
  8.8 6.0 %stack.3 = bf16[32,256,1024]{2,1,0:T(8,128)(2,1)} broadcast(bf16[256,1024]{1,0:T(8,128)(2,1)S(1)} %bitcast.19), dimensions={1,2} | broadcast | bytes 17301504 | tf_op jit(solution)/shard_map/stack | solution.py:21
  14.8 0.0 copy-start
  14.8 9.5 %all-to-all-start = ((bf16[32,256,1024]{2,1,0:T(8,128)(2,1)}), bf16[32,256,1024]{2,1,0:T(8,128)(2,1)}, u32[]{:S(2)}, u32[]{:S(2)}) async-start(bf16[32,256,1024]{2,1,0:T(8,128)(2,1)} %stack.3), calls=%async_computation | async-start | bytes 33554432 | tf_op jit(solution)/shard_map/all_to_all | solution.py:22
  24.2 0.0 reduce-scatter.2.cloned.1.call-start
  24.3 0.0 copy-done
  24.3 306.3 %all-to-all-done = bf16[32,256,1024]{2,1,0:T(8,128)(2,1)} async-done(((bf16[32,256,1024]{2,1,0:T(8,128)(2,1)}), bf16[32,256,1024]{2,1,0:T(8,128)(2,1)}, u32[]{:S(2)}, u32[]{:S(2)}) %all-to-all-start) | async-done | bytes 16777248 | tf_op jit(solution)/shard_map/all_to_all | solution.py:22
  330.6 6.5 %mul.11 = bf16[8,128,64,128]{3,2,1,0:T(8,128)(2,1)} broadcast(bf16[8,64]{1,0:T(8,128)(2,1)S(1)} %convert_element_type.15), dimensions={0,2} | broadcast | bytes 16778240 | tf_op jit(solution)/shard_map/mul | solution.py:27
  337.1 29.5 %fusion = f32[1024,1024]{1,0:T(8,128)} fusion(bf16[8192,1024]{1,0:T(8,128)(2,1)} %bitcast.2, bf16[1024,8192]{1,0:T(8,128)(2,1)} %param.4, bf16[128,8,64,128]{3,2,1,0:T(8,128)(2,1)} %bitcast.18), kind=kOutput, calls=%fused_computation.1 | convolution fusion | flops 17188257792 | bytes 54525952 | tf_op jit(solution)/shard_map/dot_general | solution.py:31
  366.5 0.0 reduce-scatter.2.cloned.1.call-update
  366.6 80.7 %reduce-scatter.2.cloned.1.call-done = f32[256,1024]{1,0:T(8,128)} async-done(((f32[1024,1024]{1,0:T(8,128)}), f32[256,1024]{1,0:T(8,128)}) %reduce-scatter.2.cloned.1.call-update) | async-done | bytes 1048592 | tf_op jit(solution)/shard_map/reduce_scatter | solution.py:34
  447.3 2.1 convert_element_type.16
  (1 shorter events, 0.0 us)
Async XLA Ops:
  14.8 9.5 %copy-start = (s32[8,64]{1,0:T(8,128)S(1)}, s32[8,64]{1,0:T(8,128)}, u32[]{:S(2)}) copy-start(s32[8,64]{1,0:T(8,128)} %param.5) | copy-start | bytes 6148
  14.8 315.8 %all-to-all-start = ((bf16[32,256,1024]{2,1,0:T(8,128)(2,1)}), bf16[32,256,1024]{2,1,0:T(8,128)(2,1)}, u32[]{:S(2)}, u32[]{:S(2)}) async-start(bf16[32,256,1024]{2,1,0:T(8,128)(2,1)} %stack.3), calls=%async_computation | async-start | bytes 33554432 | tf_op jit(solution)/shard_map/all_to_all | solution.py:22
  24.2 423.1 %reduce-scatter.2.cloned.1.call-start = ((), (), s32[]{:S(2)}) async-start(), calls=%async_computation.2 | async-start | bytes 5242880 | tf_op jit(solution)/shard_map/reduce_scatter | solution.py:34
Sparse Core Ops, SparseCore 0:
  366.7 80.5 reduce-scatter.1
